TPU v7x, 32 devices: a whole 2x2x4 slice. The times are simulated.
32 devices in a mesh: batch: 4 (over z), seq: 2 (over core), ch: 4 (over y, x).
Axes of the slice: x: 2, y: 2, z: 4, core: 2. Of those that a mesh axis runs over, the one named last changes fastest.
Arguments:
- inputs: bfloat16 [16, 1280, 2048], P('batch', 'ch', 'seq'), may hold values from -6 to 6
- segment_ids: int32 [16, 2048], P('batch', 'seq'), may hold values from 0 to 7, never falling along the last dimension, each value on 1 to 512 neighbouring positions
- norm0_gain: float32 [1280], P('ch'), may hold values from 0.1 to 1.9
- norm0_shift: float32 [1280], P('ch'), may hold values from -3 to 3
- w_inner: bfloat16 [1280, 640], P('ch'), may hold values from -0.15625 to 0.15625
- b_inner: float32 [640], P('ch'), may hold values from -3 to 3
- norm1_gain: float32 [640], P('ch'), may hold values from 0.1 to 1.9
- norm1_shift: float32 [640], P('ch'), may hold values from -3 to 3
- w_conv: bfloat16 [5, 640, 640], P(None, 'ch'), may hold values from -0.109375 to 0.109375
- b_conv: float32 [640], P('ch'), may hold values from -3 to 3
- norm2_gain: float32 [640], P('ch'), may hold values from 0.1 to 1.9
- norm2_shift: float32 [640], P('ch'), may hold values from -3 to 3
- w_outer: bfloat16 [640, 1280], P('ch'), may hold values from -0.25 to 0.25
- b_outer: float32 [1280], P('ch'), may hold values from -3 to 3
- cotangent: bfloat16 [16, 1280, 2048], P('batch', 'ch', 'seq'), may hold values from -6 to 6
Outputs:
- output: bfloat16 [16, 1280, 2048], P('batch', 'ch', 'seq')
- input_grad: bfloat16 [16, 1280, 2048], P('batch', 'ch', 'seq')
- grad_norm0_gain: float32 [1280], P('ch')
- grad_norm0_shift: float32 [1280], P('ch')
- grad_w_inner: float32 [1280, 640], P('ch')
- grad_b_inner: float32 [640], P('ch')
- grad_norm1_gain: float32 [640], P('ch')
- grad_norm1_shift: float32 [640], P('ch')
- grad_w_conv: float32 [5, 640, 640], P(None, 'ch')
- grad_b_conv: float32 [640], P('ch')
- grad_norm2_gain: float32 [640], P('ch')
- grad_norm2_shift: float32 [640], P('ch')
- grad_w_outer: float32 [640, 1280], P('ch')
- grad_b_outer: float32 [1280], P('ch')
Inputs may be any that keep to these rules, and one draw needn't show every extreme that they name: `segment_ids`: along a row the ids never fall; each protein is one run of 1 to 512 residues, one run of each row has exactly 512, and every row holds all 8 ids.
All inputs are finite; a program needn't handle non-finite values.
Results may differ from a plain program's by a relative error of at most 0.0065.
Values may be sent and summed in bfloat16 or wider, within the bound.
A program may use at most 192 MiB of HBM per device.

v0:
```python
import jax
import jax.numpy as jnp
from jax import lax
from jax.sharding import PartitionSpec as P

KERNEL_TAPS = 5
DILATION_SPACING = 32
EPSILON = 1e-05


def gelu_exact(values):
    return jax.nn.gelu(values, approximate=False)


def gelu_back(point, grad):
    return jax.vjp(gelu_exact, point)[1](grad)[0]


def normalize(values, gain, shift):
    center = jnp.mean(values, axis=1, keepdims=True)
    offset = values - center
    spread = jnp.mean(offset * offset, axis=1, keepdims=True)
    scale = lax.rsqrt(spread + EPSILON)
    unit = offset * scale
    return (unit * gain[:, None] + shift[:, None], unit, scale)


def normalize_back(grad, unit, scale, gain):
    scaled = grad * gain[:, None]
    first = jnp.mean(scaled, axis=1, keepdims=True)
    second = jnp.mean(scaled * unit, axis=1, keepdims=True)
    return scale * (scaled - first - unit * second)


def neighbour_pairs(seqs, nch, q_count):
    pairs = []
    for s in range(seqs):
        for c in range(nch):
            q = c % q_count
            if q < q_count - 1:
                pairs.append((s * nch + c, s * nch + c + 1))
            elif s < seqs - 1:
                pairs.append((s * nch + c, (s + 1) * nch + c - (q_count - 1)))
    return pairs


def extended(x, width, pairs):
    down = [(j, i) for i, j in pairs]
    length = x.shape[-1]
    before = lax.ppermute(x[..., length - width :], ("seq", "ch"), pairs)
    after = lax.ppermute(x[..., :width], ("seq", "ch"), down)
    return jnp.concatenate([before, x, after], axis=-1)


def shifted_taps(wide, wide_ids, own_ids, offsets, border):
    length = own_ids.shape[-1]
    pieces = []
    for offset in offsets:
        lower = border + offset
        shifted = wide[:, :, lower : lower + length]
        matching = wide_ids[:, lower : lower + length] == own_ids
        pieces.append(jnp.where(matching[:, None, :], shifted, jnp.zeros_like(shifted)))
    return jnp.concatenate(pieces, axis=1)


def to_positions(x, nch, q_count):
    rows, width, length = x.shape
    if q_count > 1:
        x = x.reshape(rows, width, q_count, length // q_count).transpose(0, 2, 1, 3)
        x = x.reshape(rows * q_count, width, length // q_count)
    return lax.all_to_all(x, "ch", 0, 1, tiled=True)


def to_channels(x, nch, q_count, rows):
    x = lax.all_to_all(x, "ch", 1, 0, tiled=True)
    if q_count > 1:
        _, width, part = x.shape
        x = (
            x.reshape(rows, q_count, width, part)
            .transpose(0, 2, 1, 3)
            .reshape(rows, width, q_count * part)
        )
    return x


def local(
    inputs,
    segment_ids,
    norm0_gain,
    norm0_shift,
    w_inner,
    b_inner,
    norm1_gain,
    norm1_shift,
    w_conv,
    b_conv,
    norm2_gain,
    norm2_shift,
    w_outer,
    b_outer,
    cotangent,
):
    nch = lax.axis_size("ch")
    seqs = lax.axis_size("seq")
    batches = lax.axis_size("batch")
    rows, dloc, length = inputs.shape
    hloc = w_conv.shape[1]
    hid = hloc * nch
    dim = dloc * nch
    if rows % nch == 0:
        q_count = 1
    else:
        q_count = nch // rows
    part = length // q_count
    border = 2 * DILATION_SPACING
    offsets = [(k - KERNEL_TAPS // 2) * DILATION_SPACING for k in range(KERNEL_TAPS)]
    back_offsets = [-o for o in offsets]
    pairs = neighbour_pairs(seqs, nch, q_count)
    me = lax.axis_index("ch")
    smalls = [
        norm0_gain,
        norm0_shift,
        b_inner,
        norm1_gain,
        norm1_shift,
        b_conv,
        norm2_gain,
        norm2_shift,
        b_outer,
    ]
    small_all = lax.all_gather(jnp.concatenate(smalls), "ch", axis=0, tiled=False)
    cut = 0
    full = []
    for s in smalls:
        n = s.shape[0]
        full.append(small_all[:, cut : cut + n].reshape(n * nch))
        cut += n
    g0, s0, b_in, g1, s1, b_cv, g2, s2, b_out = full
    packed = jnp.concatenate([w_inner.reshape(-1), w_conv.reshape(-1), w_outer.reshape(-1)])
    packed_all = lax.all_gather(packed.reshape(1, -1, 128), "ch", axis=0, tiled=True).reshape(
        nch, -1
    )
    n_in, n_cv = (w_inner.size, w_conv.size)
    w_in = packed_all[:, :n_in].reshape(dim, hid)
    w_cv = (
        packed_all[:, n_in : n_in + n_cv]
        .reshape(nch, KERNEL_TAPS, hloc, hid)
        .transpose(1, 0, 2, 3)
        .reshape(KERNEL_TAPS, hid, hid)
    )
    w_out = packed_all[:, n_in + n_cv :].reshape(hid, dim)
    x = to_positions(inputs, nch, q_count)
    cot = to_positions(cotangent, nch, q_count)
    prow = x.shape[0]
    if q_count == 1:
        ids = lax.dynamic_slice_in_dim(segment_ids, me * prow, prow, axis=0)
    else:
        ids = lax.dynamic_slice_in_dim(segment_ids, me // q_count, 1, axis=0)
        ids = lax.dynamic_slice_in_dim(ids, me % q_count * part, part, axis=1)
    own_ids = ids + 1
    wide_ids = extended(own_ids, border, pairs)
    residual = x.astype(jnp.float32)
    normed0, unit0, scale0 = normalize(residual, g0, s0)
    hidden0 = gelu_exact(normed0).astype(jnp.bfloat16)
    inner = (
        jnp.einsum("dh,rdl->rhl", w_in, hidden0, preferred_element_type=jnp.float32) + b_in[:, None]
    )
    normed1, unit1, scale1 = normalize(inner, g1, s1)
    hidden1 = gelu_exact(normed1).astype(jnp.bfloat16)
    wide_hidden = extended(hidden1, border, pairs)
    taps = shifted_taps(wide_hidden, wide_ids, own_ids, offsets, border)
    kernel_flat = w_cv.reshape(KERNEL_TAPS * hid, hid)
    mixed = (
        jnp.einsum("co,rcl->rol", kernel_flat, taps, preferred_element_type=jnp.float32)
        + b_cv[:, None]
    )
    normed2, unit2, scale2 = normalize(mixed, g2, s2)
    hidden2 = gelu_exact(normed2).astype(jnp.bfloat16)
    branch = jnp.einsum("hd,rhl->rdl", w_out, hidden2, preferred_element_type=jnp.float32)
    output = (residual + branch + b_out[:, None]).astype(jnp.bfloat16)
    grad_b_outer = jnp.sum(cot.astype(jnp.float32), axis=(0, 2))
    grad_w_outer = jnp.einsum("rhl,rdl->hd", hidden2, cot, preferred_element_type=jnp.float32)
    grad_hidden2 = jnp.einsum("hd,rdl->rhl", w_out, cot, preferred_element_type=jnp.float32)
    grad_normed2 = gelu_back(normed2, grad_hidden2)
    grad_norm2_gain = jnp.sum(grad_normed2 * unit2, axis=(0, 2))
    grad_norm2_shift = jnp.sum(grad_normed2, axis=(0, 2))
    grad_mixed = normalize_back(grad_normed2, unit2, scale2, g2).astype(jnp.bfloat16)
    grad_b_conv = jnp.sum(grad_mixed.astype(jnp.float32), axis=(0, 2))
    grad_w_conv = jnp.einsum(
        "rcl,rol->co", taps, grad_mixed, preferred_element_type=jnp.float32
    ).reshape(KERNEL_TAPS, hid, hid)
    wide_grad = extended(grad_mixed, border, pairs)
    back_taps = shifted_taps(wide_grad, wide_ids, own_ids, back_offsets, border)
    kernel_back = jnp.transpose(w_cv, (0, 2, 1)).reshape(KERNEL_TAPS * hid, hid)
    grad_hidden1 = jnp.einsum(
        "oc,rol->rcl", kernel_back, back_taps, preferred_element_type=jnp.float32
    )
    grad_normed1 = gelu_back(normed1, grad_hidden1)
    grad_norm1_gain = jnp.sum(grad_normed1 * unit1, axis=(0, 2))
    grad_norm1_shift = jnp.sum(grad_normed1, axis=(0, 2))
    grad_inner = normalize_back(grad_normed1, unit1, scale1, g1).astype(jnp.bfloat16)
    grad_b_inner = jnp.sum(grad_inner.astype(jnp.float32), axis=(0, 2))
    grad_w_inner = jnp.einsum(
        "rdl,rhl->dh", hidden0, grad_inner, preferred_element_type=jnp.float32
    )
    grad_hidden0 = jnp.einsum("dh,rhl->rdl", w_in, grad_inner, preferred_element_type=jnp.float32)
    grad_normed0 = gelu_back(normed0, grad_hidden0)
    grad_norm0_gain = jnp.sum(grad_normed0 * unit0, axis=(0, 2))
    grad_norm0_shift = jnp.sum(grad_normed0, axis=(0, 2))
    input_grad = (cot.astype(jnp.float32) + normalize_back(grad_normed0, unit0, scale0, g0)).astype(
        jnp.bfloat16
    )
    output = to_channels(output, nch, q_count, rows)
    input_grad = to_channels(input_grad, nch, q_count, rows)
    grads = [
        grad_norm0_gain,
        grad_norm0_shift,
        grad_w_inner,
        grad_b_inner,
        grad_norm1_gain,
        grad_norm1_shift,
        grad_w_conv.transpose(1, 0, 2),
        grad_b_conv,
        grad_norm2_gain,
        grad_norm2_shift,
        grad_w_outer,
        grad_b_outer,
    ]
    flat = [g.reshape(nch, -1) for g in grads]
    sizes = [f.shape[1] for f in flat]
    stack = jnp.concatenate(flat, axis=1)
    total = stack.shape[1]
    lanes = 128
    spread = seqs * batches * 8 * lanes
    padded = -(-total // spread) * spread
    if padded != total:
        stack = jnp.pad(stack, ((0, 0), (0, padded - total)))
    stack = stack.reshape(nch, padded // lanes, lanes)
    stack = lax.psum_scatter(stack, "seq", scatter_dimension=1, tiled=True)
    stack = lax.psum_scatter(stack, "batch", scatter_dimension=1, tiled=True)
    stack = lax.psum_scatter(stack, "ch", scatter_dimension=0, tiled=True)
    stack = lax.all_gather(stack, ("seq", "batch"), axis=1, tiled=True).reshape(padded)[:total]
    shard_shapes = [
        norm0_gain.shape,
        norm0_shift.shape,
        w_inner.shape,
        b_inner.shape,
        norm1_gain.shape,
        norm1_shift.shape,
        (hloc, KERNEL_TAPS, hid),
        b_conv.shape,
        norm2_gain.shape,
        norm2_shift.shape,
        w_outer.shape,
        b_outer.shape,
    ]
    outs = []
    cut = 0
    for n, shape in zip(sizes, shard_shapes):
        outs.append(stack[cut : cut + n].reshape(shape))
        cut += n
    outs[6] = outs[6].transpose(1, 0, 2)
    return (output, input_grad, *outs)


def solution(mesh):
    return jax.shard_map(
        local,
        mesh=mesh,
        in_specs=(
            P("batch", "ch", "seq"),
            P("batch", "seq"),
            P("ch"),
            P("ch"),
            P("ch", None),
            P("ch"),
            P("ch"),
            P("ch"),
            P(None, "ch", None),
            P("ch"),
            P("ch"),
            P("ch"),
            P("ch", None),
            P("ch"),
            P("batch", "ch", "seq"),
        ),
        out_specs=(
            P("batch", "ch", "seq"),
            P("batch", "ch", "seq"),
            P("ch"),
            P("ch"),
            P("ch", None),
            P("ch"),
            P("ch"),
            P("ch"),
            P(None, "ch", None),
            P("ch"),
            P("ch"),
            P("ch"),
            P("ch", None),
            P("ch"),
        ),
        check_vma=False,
    )
```

profile of v0, /device:TPU:0, one launch (start us, length us, event | category | flops | bytes accessed | tf_op | source)
XLA Modules:
  0.0 816.1 jit_solution(5555885793643184578)
XLA Ops:
  10.0 1.8 reshape.1466
  13.4 5.3 all-to-all-start
  22.4 49.7 %all-gather.1 = f32[4,1,1920]{2,1,0:T(1,128)S(1)} all-gather(f32[1,1,1920]{2,1,0:T(1,128)S(1)} %reshape.1500), channel_id=2, replica_groups=mesh['batch'=4,'seq'=2,'ch'=4] {'ch'}, dimensions={0}, use_global_device_ids=true | all-gather | bytes 38400 | tf_op jit(solution)/shard_map/all_gather | solution.py:131
  73.7 4.8 all-to-all-start.2
  81.5 14.8 %fusion.6 = bf16[1,1280,1,1,1,1,1024]{6,1,5,4,3,2,0:T(8,128)(2,1)} fusion(f32[1,1280,1,1,1,1,1024]{6,1,5,4,3,2,0:T(8,128)S(1)} %bitcast.270, f32[1280]{0:T(1024)S(1)} %add.153, f32[1280]{0:T(1024)S(1)} %mul.431, f32[1024]{0:T(1024)S(1)} %add_rsqrt_fusion.2, f32[1024]{0:T(1024)S(1)} %broadcast_multiply_fusion.8), kind=kLoop, calls=%fused_computation.11 | loop fusion | flops 90439680 | bytes 7882752 | tf_op jit(solution)/shard_map/convert_element_type | solution.py:164
  96.3 48.7 %all-gather.5.cloned.1.call-done = bf16[4,7200,128]{2,1,0:T(8,128)(2,1)} async-done(((bf16[1,7200,128]{2,1,0:T(8,128)(2,1)}), bf16[4,7200,128]{2,1,0:T(8,128)(2,1)}) %all-gather.5.cloned.1.call-update) | async-done | bytes 7372816 | tf_op jit(solution)/shard_map/all_gather | solution.py:140
  145.0 26.1 %copy.86 = bf16[1,4,7200,128]{3,1,2,0:T(4,128)(2,1)S(1)} copy(bf16[1,4,7200,128]{3,2,1,0:T(8,128)(2,1)} %bitcast.283) | data formatting | bytes 14745600
  171.1 3.0 copy-done.6
  174.0 2.0 fusion.110
  176.1 2.3 reshape.1470
  178.4 4.5 fusion.72
  183.5 7.3 multiply_convert_fusion.1
  191.8 1.9 collective-permute-start.1
  193.8 2.7 convert_reduce_fusion.3
  196.5 5.9 copy.61
  202.4 3.6 slice.212
  206.6 2.4 copy.60
  208.9 4.1 reshape.1474
  214.3 7.9 copy.66
  222.2 2.9 fusion.90
  226.6 8.0 constant_dynamic-update-slice_fusion
  237.5 9.6 %copy.69 = bf16[1,3200,1024]{2,1,0:T(8,128)(2,1)} copy(bf16[1,3200,1024]{1,2,0:T(8,128)(2,1)} %fusion.97) | data formatting | bytes 13107200 | tf_op jit(solution)/shard_map/concatenate | solution.py:63
  247.0 9.1 %fusion.74 = (f32[1024]{0:T(1024)S(1)}, f32[1024,640]{1,0:T(8,128)S(1)}) fusion(f32[640]{0:T(1024)S(1)} %add.163, bf16[3200,640]{1,0:T(8,128)(2,1)} %bitcast.279, bf16[1,3200,1024]{1,2,0:T(8,128)(2,1)} %fusion.97), kind=kOutput, calls=%fused_computation.146 | convolution fusion | flops 4195613696 | bytes 13277696 | tf_op jit(solution)/shard_map/co,rcl->rol/dot_general | solution.py:174
  256.7 11.8 %fusion.105 = f32[640,1280]{1,0:T(8,128)} fusion(bf16[1280,1024]{1,0:T(8,128)(2,1)} %bitcast.15, f32[640]{0:T(1024)S(1)} %add.167, f32[640]{0:T(1024)S(1)} %mul.451, f32[1024]{0:T(1024)S(1)} %add_rsqrt_fusion, f32[1024]{0:T(1024)S(1)} %broadcast_multiply_fusion.4, f32[640]{0:T(1024)S(1)} %add.163, f32[1024,640]{1,0:T(8,128)S(1)} %get-tuple-element.121), kind=kOutput, calls=%fused_computation.218 | convolution fusion | flops 1723596800 | bytes 8535552 | tf_op jit(solution)/shard_map/rhl,rdl->hd/dot_general | solution.py:182
  268.6 12.4 %fusion.50 = (f32[640]{0:T(1024)S(1)}, f32[1024]{0:T(1024)S(1)}, f32[1024]{0:T(1024)S(1)}, f32[640]{0:T(1024)S(1)}, f32[1,640,1024]{1,2,0:T(8,128)}) fusion(f32[1024]{0:T(1024)S(1)} %add_rsqrt_fusion, f32[1024]{0:T(1024)S(1)} %broadcast_multiply_fusion.4, f32[640]{0:T(1024)S(1)} %add.163, f32[1024,640]{1,0:T(8,128)S(1)} %get-tuple-element.121, ...), kind=kOutput, calls=%fused_computation.93 | convolution fusion | flops 1732113152 | bytes 9531904 | tf_op jit(solution)/shard_map/hd,rdl->rhl/dot_general | solution.py:183
  281.1 3.1 convert_reduce_fusion.1
  284.3 5.2 reshape.1491
  289.5 3.0 collective-permute-start.5
  293.9 7.6 convolution_bitcast_fusion
  301.4 9.7 %copy.71 = f32[640,5,640]{2,1,0:T(8,128)} copy(f32[640,5,640]{2,0,1:T(8,128)S(1)} %convolution_bitcast_fusion) | data formatting | bytes 16384000 | tf_op jit(solution)/shard_map/transpose | solution.py:222
  311.2 12.0 %reshape.1487 = f32[4,512000]{1,0:T(4,128)} reshape(f32[640,5,640]{2,1,0:T(8,128)} %copy.71) | data formatting | bytes 16384000 | tf_op jit(solution)/shard_map/reshape | solution.py:229
  326.9 13.5 %fusion.56 = (f32[640]{0:T(1024)S(1)}, f32[1024]{0:T(1024)S(1)}, f32[1024]{0:T(1024)S(1)}, f32[640]{0:T(1024)S(1)}, f32[1,640,1024]{1,2,0:T(8,128)}) fusion(f32[1024]{0:T(1024)S(1)} %add_rsqrt_fusion.1, f32[1024]{0:T(1024)S(1)} %broadcast_multiply_fusion.5, f32[640]{0:T(1024)S(1)} %add.156, f32[1024,640]{1,0:T(8,128)S(1)} %copy-done.2, f32[640]{0:T(1024)S(1)} %mul.441, ...), kind=kOutput, calls=%fused_computation.104 | convolution fusion | flops 4248695808 | bytes 15921664 | tf_op jit(solution)/shard_map/oc,rol->rcl/dot_general | solution.py:195
  340.5 3.3 convert_reduce_fusion.2
  343.9 6.0 fusion.57
  349.9 3.5 reshape.1482
  353.4 19.2 %multiply_reduce_fusion = (f32[1280]{0:T(1024)S(1)}, f32[1024]{0:T(1024)S(1)}, f32[1024]{0:T(1024)S(1)}, f32[1280]{0:T(1024)S(1)}, f32[1,1280,1024]{1,2,0:T(8,128)}) fusion(f32[1,1280,1024]{1,2,0:T(8,128)} %copy.61, f32[1024]{0:T(1024)S(1)} %copy-done.15, f32[1024]{0:T(1024)S(1)} %copy-done.17, f32[1280]{0:T(1024)S(1)} %copy-done.13, ...), kind=kOutput, calls=%fused_computation.24 | convolution fusion | flops 1785196032 | bytes 13471744 | tf_op jit(solution)/shard_map/dh,rhl->rdl/dot_general | solution.py:206
  375.6 1.8 constant_dynamic-update-slice_fusion.2
  381.6 43.2 %dynamic-update-slice.6 = f32[4,923520]{1,0:T(4,128)} dynamic-update-slice(f32[4,923520]{1,0:T(4,128)} %dynamic-update-slice.5, f32[4,512000]{1,0:T(4,128)} %reshape.1487, s32[]{} %constant.29, s32[]{} %constant.35) | dynamic-update-slice | bytes 16384004
  426.2 1.7 dynamic-update-slice.8
  429.4 17.2 %dynamic-update-slice.10 = f32[4,923520]{1,0:T(4,128)} dynamic-update-slice(f32[4,923520]{1,0:T(4,128)} %dynamic-update-slice.9, f32[4,204800]{1,0:T(4,128)S(1)} %copy-done.7, s32[]{} %constant.29, s32[]{} %constant.146) | dynamic-update-slice | bytes 6553604
  448.0 12.8 %pad_bitcast_fusion = f32[1,4,7232,128]{3,1,2,0:T(4,128)} fusion(f32[4,923520]{1,0:T(4,128)} %dynamic-update-slice.11), kind=kLoop, calls=%fused_computation.1 | loop fusion | bytes 29587456
  460.8 11.4 %copy.85 = f32[1,4,7232,128]{3,2,1,0:T(8,128)} copy(f32[1,4,7232,128]{3,1,2,0:T(4,128)} %pad_bitcast_fusion) | data formatting | bytes 29622272
  472.2 24.9 %reduce-scatter.6.cloned.1.call-done = f32[4,3616,128]{2,1,0:T(8,128)} async-done(((f32[4,7232,128]{2,1,0:T(8,128)}), f32[4,3616,128]{2,1,0:T(8,128)}) %reduce-scatter.6.cloned.1.call-update) | async-done | bytes 7405584 | tf_op jit(solution)/shard_map/reduce_scatter | solution.py:239
  497.2 132.5 %reduce-scatter.8.cloned.1.call-done = f32[4,904,128]{2,1,0:T(8,128)} async-done(((f32[4,3616,128]{2,1,0:T(8,128)}), f32[4,904,128]{2,1,0:T(8,128)}) %reduce-scatter.8.cloned.1.call-update) | async-done | bytes 1851408 | tf_op jit(solution)/shard_map/reduce_scatter | solution.py:240
  629.7 37.5 %reduce-scatter.10.cloned.1.call-done = f32[1,904,128]{2,1,0:T(8,128)} async-done(((f32[4,904,128]{2,1,0:T(8,128)}), f32[1,904,128]{2,1,0:T(8,128)}) %reduce-scatter.10.cloned.1.call-update) | async-done | bytes 462864
  667.3 11.7 %fusion.12 = bf16[1,1280,1024]{1,2,0:T(8,128)(2,1)} fusion(f32[1,1280,1024]{1,2,0:T(8,128)} %copy.61, bf16[640,1280]{1,0:T(8,128)(2,1)} %reshape.1474, f32[1280]{0:T(1024)S(1)} %add.171, f32[640]{0:T(1024)S(1)} %add.167, f32[640]{0:T(1024)S(1)} %mul.451, f32[1024]{0:T(1024)S(1)} %add_rsqrt_fusion, f32[1024]{0:T(1024)S(1)} %broadcast_multiply_fusion.4, ...), kind=kOutput, calls=%fused_computation.18 | convolution fusion | flops 1727528960 | bytes 12145152 | tf_op jit(solution)/shard_map/hd,rhl->rdl/dot_general | solution.py:179
  679.0 11.6 %copy.62 = bf16[1,1280,1024]{2,0,1:T(2,128)(2,1)} copy(bf16[1,1280,1024]{1,2,0:T(8,128)(2,1)} %fusion.12) | data formatting | bytes 5242880 | tf_op jit(solution)/shard_map/convert_element_type | solution.py:180
  691.1 15.6 %reduce.29 = bf16[1280,1024]{1,0:T(8,128)(2,1)S(1)} reduce(bf16[1280,1,1024]{2,1,0:T(2,128)(2,1)} %bitcast.274, bf16[]{:T(256)} %broadcast.2394), dimensions={1}, to_apply=%bitcast.237.reduce_sub_computation | reduce | bytes 5242882
  706.7 3.1 reshape.1509
  709.9 4.6 all-to-all-start.1
  714.4 4.9 copy.67
  719.4 6.4 add_convert_fusion
  725.8 8.3 %copy.68 = bf16[1,1280,1024]{2,0,1:T(2,128)(2,1)} copy(bf16[1,1280,1024]{1,2,0:T(8,128)(2,1)S(1)} %add_convert_fusion) | data formatting | bytes 5242880 | tf_op jit(solution)/shard_map/convert_element_type | solution.py:210
  734.0 15.6 %reduce.30 = bf16[1280,1024]{1,0:T(8,128)(2,1)S(1)} reduce(bf16[1280,1,1024]{2,1,0:T(2,128)(2,1)} %bitcast.275, bf16[]{:T(256)} %broadcast.2394), dimensions={1}, to_apply=%bitcast.239.reduce_sub_computation | reduce | bytes 5242882
  749.6 3.2 reshape.1511
  752.8 4.3 all-to-all-start.3
  757.1 5.5 reshape.1510
  762.7 5.0 copy.77
  767.7 19.7 %all-to-all-done.3 = bf16[4,2,163840]{2,1,0:T(2,128)(2,1)S(1)} async-done(((bf16[4,2,163840]{2,1,0:T(2,128)(2,1)}), bf16[4,2,163840]{2,1,0:T(2,128)(2,1)S(1)}, u32[]{:S(2)}, u32[]{:S(2)}) %all-to-all-start.3) | async-done | bytes 2621472 | tf_op jit(solution)/shard_map/all_to_all | solution.py:75
  787.3 3.8 reshape.1512
  791.2 5.0 copy.78
  796.2 2.3 slice_bitcast_fusion
  800.1 1.9 slice.231
  805.2 2.4 reshape.1494
  (157 shorter events, 45.0 us)
Async XLA Ops:
  7.2 137.8 %all-gather.5.cloned.1.call-start = ((), (), s32[]{:S(2)}) async-start(), calls=%async_computation.7 | async-start | bytes 9216000 | tf_op jit(solution)/shard_map/all_gather | solution.py:140
  13.2 9.0 %copy-start.22 = (f32[320]{0:T(512)S(1)}, f32[320]{0:T(512)}, u32[]{:S(2)}) copy-start(f32[320]{0:T(512)} %param.17) | copy-start | bytes 3844
  13.3 9.0 %copy-start.23 = (f32[320]{0:T(512)S(1)}, f32[320]{0:T(512)}, u32[]{:S(2)}) copy-start(f32[320]{0:T(512)} %param.18) | copy-start | bytes 3844
  13.3 9.0 %copy-start.24 = (f32[320]{0:T(512)S(1)}, f32[320]{0:T(512)}, u32[]{:S(2)}) copy-start(f32[320]{0:T(512)} %param.28) | copy-start | bytes 3844
  13.3 9.0 %copy-start.25 = (f32[160]{0:T(256)S(1)}, f32[160]{0:T(256)}, u32[]{:S(2)}) copy-start(f32[160]{0:T(256)} %param.20) | copy-start | bytes 1924
  13.3 9.0 %copy-start.26 = (f32[160]{0:T(256)S(1)}, f32[160]{0:T(256)}, u32[]{:S(2)}) copy-start(f32[160]{0:T(256)} %param.21) | copy-start | bytes 1924
  13.3 9.0 %copy-start.27 = (f32[160]{0:T(256)S(1)}, f32[160]{0:T(256)}, u32[]{:S(2)}) copy-start(f32[160]{0:T(256)} %param.22) | copy-start | bytes 1924
  13.3 9.0 %copy-start.28 = (f32[160]{0:T(256)S(1)}, f32[160]{0:T(256)}, u32[]{:S(2)}) copy-start(f32[160]{0:T(256)} %param.24) | copy-start | bytes 1924
  13.3 9.0 %copy-start.29 = (f32[160]{0:T(256)S(1)}, f32[160]{0:T(256)}, u32[]{:S(2)}) copy-start(f32[160]{0:T(256)} %param.25) | copy-start | bytes 1924
  13.3 9.0 %copy-start.30 = (f32[160]{0:T(256)S(1)}, f32[160]{0:T(256)}, u32[]{:S(2)}) copy-start(f32[160]{0:T(256)} %param.26) | copy-start | bytes 1924
  13.4 60.4 %all-to-all-start = ((bf16[4,320,1024]{2,1,0:T(8,128)(2,1)}), bf16[4,320,1024]{2,1,0:T(8,128)(2,1)S(1)}, u32[]{:S(2)}, u32[]{:S(2)}) async-start(bf16[4,320,1024]{2,1,0:T(8,128)(2,1)} %param.15), calls=%async_computation | async-start | bytes 5242880 | tf_op jit(solution)/shard_map/all_to_all | solution.py:71
  19.5 54.1 %collective-permute-start = (s32[1,64]{1,0:T(1,128)S(1)}, s32[1,64]{1,0:T(1,128)S(1)}, u32[]{:S(2)}, u32[]{:S(2)}) collective-permute-start(s32[1,64]{1,0:T(1,128)S(1)} %get-tuple-element.116), channel_id=1, source_target_pairs={{0,4},{1,5},{2,6},{3,7},{8,12},{9,13},{10,14},{11,15},{16,20},{17,... | collective-permute-start | bytes 776 | tf_op jit(solution)/shard_map/ppermute | solution.py:50
  20.9 52.6 %collective-permute-start.2 = (s32[1,64]{1,0:T(1,128)S(1)}, s32[1,64]{1,0:T(1,128)S(1)}, u32[]{:S(2)}, u32[]{:S(2)}) collective-permute-start(s32[1,64]{1,0:T(1,128)S(1)} %get-tuple-element.117), channel_id=1, source_target_pairs={{4,0},{5,1},{6,2},{7,3},{12,8},{13,9},{14,10},{15,11},{20,16},{21,... | collective-permute-start | bytes 776 | tf_op jit(solution)/shard_map/ppermute | solution.py:51
  73.1 7.3 copy-start.12
  73.6 6.9 copy-start.18
  73.7 120.1 %all-to-all-start.2 = ((bf16[4,320,1024]{2,1,0:T(8,128)(2,1)}), bf16[4,320,1024]{2,1,0:T(8,128)(2,1)}, u32[]{:S(2)}, u32[]{:S(2)}) async-start(bf16[4,320,1024]{2,1,0:T(8,128)(2,1)} %param.29), calls=%async_computation.2 | async-start | bytes 5242880 | tf_op jit(solution)/shard_map/all_to_all | solution.py:71
  78.5 418.6 %reduce-scatter.6.cloned.1.call-start = ((), (), s32[]{:S(2)}) async-start(), calls=%async_computation.8 | async-start | bytes 22216704 | tf_op jit(solution)/shard_map/reduce_scatter | solution.py:239
  79.2 2.3 copy-start
  79.6 16.6 %copy-start.14 = (f32[1024]{0:T(1024)}, f32[1024]{0:T(1024)S(1)}, u32[]{:S(2)}) copy-start(f32[1024]{0:T(1024)S(1)} %broadcast_multiply_fusion.8) | copy-start | bytes 12292
  80.4 15.9 %copy-start.16 = (f32[1024]{0:T(1024)}, f32[1024]{0:T(1024)S(1)}, u32[]{:S(2)}) copy-start(f32[1024]{0:T(1024)S(1)} %add_rsqrt_fusion.2) | copy-start | bytes 12292
  171.0 3.0 copy-start.6
  182.9 43.6 %copy-start.1 = (f32[1024,640]{1,0:T(8,128)}, f32[1024,640]{1,0:T(8,128)S(1)}, u32[]{:S(2)}) copy-start(f32[1024,640]{1,0:T(8,128)S(1)} %get-tuple-element.119) | copy-start | bytes 7864324
  190.8 1.1 copy-start.4
  191.8 30.4 %collective-permute-start.1 = (bf16[1,640,64]{1,2,0:T(8,128)(2,1)S(1)}, bf16[1,640,64]{1,2,0:T(8,128)(2,1)S(1)}, u32[]{:S(2)}, u32[]{:S(2)}) collective-permute-start(bf16[1,640,64]{1,2,0:T(8,128)(2,1)S(1)} %get-tuple-element.106), channel_id=1, source_target_pairs={{0,4},{1,5},{2,6},{3,7},{8,12},{9,13},{10,14},{11,15},{16,20},{17,... | collective-permute-start | bytes 245768 | tf_op jit(solution)/shard_map/ppermute | solution.py:50
  213.1 21.5 %collective-permute-start.3 = (bf16[1,640,64]{1,2,0:T(8,128)(2,1)S(1)}, bf16[1,640,64]{1,2,0:T(8,128)(2,1)S(1)}, u32[]{:S(2)}, u32[]{:S(2)}) collective-permute-start(bf16[1,640,64]{1,2,0:T(8,128)(2,1)S(1)} %get-tuple-element.105), channel_id=1, source_target_pairs={{4,0},{5,1},{6,2},{7,3},{12,8},{13,9},{14,10},{15,11},{20,16},{21,... | collective-permute-start | bytes 245768 | tf_op jit(solution)/shard_map/ppermute | solution.py:51
  222.2 2.9 copy-start.5
  256.2 12.4 %copy-start.8 = (f32[1024,640]{1,0:T(8,128)}, f32[1024,640]{1,0:T(8,128)S(1)}, u32[]{:S(2)}) copy-start(f32[1024,640]{1,0:T(8,128)S(1)} %get-tuple-element.121) | copy-start | bytes 7864324
  256.7 11.8 %copy-start.11 = (bf16[640,1280]{1,0:T(8,128)(2,1)S(1)}, bf16[640,1280]{1,0:T(8,128)(2,1)}, u32[]{:S(2)}) copy-start(bf16[640,1280]{1,0:T(8,128)(2,1)} %reshape.1474) | copy-start | bytes 4915204
  289.5 34.6 %collective-permute-start.5 = (bf16[1,640,64]{1,2,0:T(8,128)(2,1)S(1)}, bf16[1,640,64]{1,2,0:T(8,128)(2,1)S(1)}, u32[]{:S(2)}, u32[]{:S(2)}) collective-permute-start(bf16[1,640,64]{1,2,0:T(8,128)(2,1)S(1)} %get-tuple-element.103), channel_id=1, source_target_pairs={{0,4},{1,5},{2,6},{3,7},{8,12},{9,13},{10,14},{11,15},{16,20},{17,... | collective-permute-start | bytes 245768 | tf_op jit(solution)/shard_map/ppermute | solution.py:50
  292.6 30.6 %collective-permute-start.4 = (bf16[1,640,64]{1,2,0:T(8,128)(2,1)S(1)}, bf16[1,640,64]{1,2,0:T(8,128)(2,1)S(1)}, u32[]{:S(2)}, u32[]{:S(2)}) collective-permute-start(bf16[1,640,64]{1,2,0:T(8,128)(2,1)S(1)} %get-tuple-element.104), channel_id=1, source_target_pairs={{4,0},{5,1},{6,2},{7,3},{12,8},{13,9},{14,10},{15,11},{20,16},{21,... | collective-permute-start | bytes 245768 | tf_op jit(solution)/shard_map/ppermute | solution.py:51
  323.9 2.2 copy-start.10
  324.1 2.8 copy-start.2
  326.9 13.6 %copy-start.3 = (f32[1024,640]{1,0:T(8,128)S(1)}, f32[1024,640]{1,0:T(8,128)}, u32[]{:S(2)}) copy-start(f32[1024,640]{1,0:T(8,128)} %copy-done.1) | copy-start | bytes 7864324
  349.9 3.5 copy-start.13
  349.9 3.5 copy-start.15
  349.9 3.5 copy-start.17
  349.9 3.5 copy-start.19
  381.6 47.8 %copy-start.7 = (f32[4,204800]{1,0:T(4,128)S(1)}, f32[4,204800]{1,0:T(4,128)}, u32[]{:S(2)}) copy-start(f32[4,204800]{1,0:T(4,128)} %reshape.1491) | copy-start | bytes 9830404
  429.4 17.3 %copy-start.21 = (f32[4,320]{1,0:T(4,128)S(1)}, f32[4,320]{1,0:T(4,128)}, u32[]{:S(2)}) copy-start(f32[4,320]{1,0:T(4,128)} %convert_reduce_fusion.3) | copy-start | bytes 15364
  472.1 157.5 %reduce-scatter.8.cloned.1.call-start = ((), (), s32[]{:S(2)}) async-start(), calls=%async_computation.9 | async-start | bytes 9256960 | tf_op jit(solution)/shard_map/reduce_scatter | solution.py:240
  497.1 170.1 %copy-start.20 = (f32[4,320]{1,0:T(4,128)S(1)}, f32[4,320]{1,0:T(4,128)}, u32[]{:S(2)}) copy-start(f32[4,320]{1,0:T(4,128)} %get-tuple-element.114) | copy-start | bytes 15364
  497.1 170.2 %copy-start.9 = (f32[1024,640]{1,0:T(8,128)S(1)}, f32[1024,640]{1,0:T(8,128)}, u32[]{:S(2)}) copy-start(f32[1024,640]{1,0:T(8,128)} %copy-done.8) | copy-start | bytes 7864324
  497.2 170.1 %reduce-scatter.10.cloned.1.call-start = ((), (), s32[]{:S(2)}) async-start(), calls=%async_computation.11 | async-start | bytes 2314240
  629.7 166.5 %all-gather.7.cloned.1.call-start = ((), (), s32[]{:S(2)}) async-start(), calls=%async_computation.10 | async-start | bytes 4165632 | tf_op jit(solution)/shard_map/all_gather | solution.py:242
  709.9 43.0 %all-to-all-start.1 = ((bf16[4,2,163840]{2,1,0:T(2,128)(2,1)}), bf16[4,2,163840]{2,1,0:T(2,128)(2,1)}, u32[]{:S(2)}, u32[]{:S(2)}) async-start(bf16[4,2,163840]{2,1,0:T(2,128)(2,1)} %reshape.1509), calls=%async_computation.1 | async-start | bytes 5242880 | tf_op jit(solution)/shard_map/all_to_all | solution.py:75
  752.8 34.5 %all-to-all-start.3 = ((bf16[4,2,163840]{2,1,0:T(2,128)(2,1)}), bf16[4,2,163840]{2,1,0:T(2,128)(2,1)S(1)}, u32[]{:S(2)}, u32[]{:S(2)}) async-start(bf16[4,2,163840]{2,1,0:T(2,128)(2,1)} %reshape.1511), calls=%async_computation.3 | async-start | bytes 5242880 | tf_op jit(solution)/shard_map/all_to_all | solution.py:75
Sparse Core Ops, SparseCore 0:
  13.4 131.5 all-gather.4
  472.3 24.8 reduce-scatter.5
  499.5 130.0 reduce-scatter.7
  632.5 34.6 reduce-scatter.9
  668.7 42.8 all-gather.6
where the time goes:
time: 824 us; the launch traced here: 816 us
  local copies, waits for them, and re-layouts  273 us (33%)
  waiting for transfers between devices  263 us (32%)
  matrix products  95.8 us (12%)
  other arithmetic  90.6 us (11%)
  blocking collectives  49.7 us (6%)
  starting transfers between devices  29.4 us (4%)
  between operations  14.6 us (2%)
    unnamed x88, local copies, waits for them, and re-layouts  160 us
    reduce_scatter x1, waiting for transfers between devices, local(): stack = lax.psum_scatter(stack, 'batch', scatter_dimension=1, tiled=True)  132 us
    all_gather x1, blocking collectives, local(): lax.all_gather(jnp.concatenate(smalls), 'ch', axis=0, tiled=False)  49.7 us
    all_gather x1, waiting for transfers between devices, local(): lax.all_gather(packed.reshape(1, -1, 128), 'ch', axis=0, tiled=True)  48.7 us
    unnamed x10, other arithmetic  46 us
    unnamed x6, waiting for transfers between devices  37.6 us
    reduce_scatter x1, waiting for transfers between devices, local(): stack = lax.psum_scatter(stack, 'seq', scatter_dimension=1, tiled=True)  24.9 us
    reshape x11, local copies, waits for them, and re-layouts, local(): flat = [g.reshape(nch, -1) for g in grads]  21.3 us
  transfers between devices with their start and end apart: 15, of which 5 were waited for; matrix products, arithmetic and copies ran while one was open for 28% of the time, Pallas kernels for 0%

commit v1 on v0

--- a/solution.py
+++ b/solution.py
@@ -72,7 +72,12 @@
 
 
 def to_channels(x, nch, q_count, rows):
-    x = lax.all_to_all(x, "ch", 1, 0, tiled=True)
+    x = jnp.concatenate(
+        jax.lax.all_to_all(
+            jnp.stack(jnp.split(x, jax.lax.axis_size("ch"), axis=1), axis=0), "ch", 0, 0
+        ),
+        axis=0,
+    )
     if q_count > 1:
         _, width, part = x.shape
         x = (

time: 824 us -> 785 us (0.953)
  local copies, waits for them, and re-layouts: 273 us -> 240 us
  other arithmetic: 90.6 us -> 61.2 us
  waiting for transfers between devices: 263 us -> 288 us
    unnamed x10 -> x8, other arithmetic: 46 us -> 14.9 us
    all_to_all x2, waiting for transfers between devices: 19.7 us -> 49.8 us  [to_channels(): jax.lax.all_to_all(jnp.stack(jnp.split(x, jax.lax.axis_size('ch'), axis=1...]
    unnamed x88 -> x87, local copies, waits for them, and re-layouts: 160 us -> 139 us
    convert_element_type x2 -> x0, local copies, waits for them, and re-layouts: 19.9 us -> none  [the longest x1 11.6 us: local(): output = (residual + branch + b_out[:, None]).astype(jnp.bfloat16)]
  transfers between devices with their start and end apart: 15 -> 15, of which waited for: 5 -> 6; matrix products, arithmetic and copies ran while one was open for 28% -> 21% of each run, Pallas kernels for 0% -> 0%
where the time goes in v1:
time: 785 us; the launch traced here: 778 us
  waiting for transfers between devices  288 us (37%)
  local copies, waits for them, and re-layouts  240 us (31%)
  matrix products  95 us (12%)
  other arithmetic  61.2 us (8%)
  blocking collectives  49.7 us (6%)
  starting transfers between devices  28.8 us (4%)
  between operations  14.9 us (2%)
    unnamed x87, local copies, waits for them, and re-layouts  139 us
    reduce_scatter x1, waiting for transfers between devices, local(): stack = lax.psum_scatter(stack, 'batch', scatter_dimension=1, tiled=True)  132 us
    all_to_all x2, waiting for transfers between devices, to_channels(): jax.lax.all_to_all(jnp.stack(jnp.split(x, jax.lax.axis_size('ch'), axis=1...  49.8 us
    all_gather x1, blocking collectives, local(): lax.all_gather(jnp.concatenate(smalls), 'ch', axis=0, tiled=False)  49.7 us
    all_gather x1, waiting for transfers between devices, local(): lax.all_gather(packed.reshape(1, -1, 128), 'ch', axis=0, tiled=True)  48.7 us
    unnamed x6, waiting for transfers between devices  32.5 us
    reduce_scatter x1, waiting for transfers between devices, local(): stack = lax.psum_scatter(stack, 'seq', scatter_dimension=1, tiled=True)  24.9 us
    reshape x11, local copies, waits for them, and re-layouts, local(): flat = [g.reshape(nch, -1) for g in grads]  21.3 us
  transfers between devices with their start and end apart: 15, of which 6 were waited for; matrix products, arithmetic and copies ran while one was open for 21% of the time, Pallas kernels for 0%

profile of v1, /device:TPU:0, one launch (start us, length us, event | category | flops | bytes accessed | tf_op | source)
XLA Modules:
  0.0 777.7 jit_solution(13455571146473707824)
XLA Ops:
  8.5 1.5 reshape.1467
  10.0 1.8 reshape.1466
  13.4 5.3 all-to-all-start
  22.4 49.7 %all-gather.1 = f32[4,1,1920]{2,1,0:T(1,128)S(1)} all-gather(f32[1,1,1920]{2,1,0:T(1,128)S(1)} %reshape.1502), channel_id=2, replica_groups=mesh['batch'=4,'seq'=2,'ch'=4] {'ch'}, dimensions={0}, use_global_device_ids=true | all-gather | bytes 38400 | tf_op jit(solution)/shard_map/all_gather | solution.py:136
  73.7 4.8 all-to-all-start.2
  81.5 14.8 %fusion.6 = bf16[1,1280,1,1,1,1,1024]{6,1,5,4,3,2,0:T(8,128)(2,1)} fusion(f32[1,1280,1,1,1,1,1024]{6,1,5,4,3,2,0:T(8,128)S(1)} %bitcast.282, f32[1280]{0:T(1024)S(1)} %add.153, f32[1280]{0:T(1024)S(1)} %mul.431, f32[1024]{0:T(1024)S(1)} %add_rsqrt_fusion.2, f32[1024]{0:T(1024)S(1)} %broadcast_multiply_fusion.8), kind=kLoop, calls=%fused_computation.11 | loop fusion | flops 90439680 | bytes 7882752 | tf_op jit(solution)/shard_map/convert_element_type | solution.py:169
  96.2 48.7 %all-gather.5.cloned.1.call-done = bf16[4,7200,128]{2,1,0:T(8,128)(2,1)} async-done(((bf16[1,7200,128]{2,1,0:T(8,128)(2,1)}), bf16[4,7200,128]{2,1,0:T(8,128)(2,1)}) %all-gather.5.cloned.1.call-update) | async-done | bytes 7372816 | tf_op jit(solution)/shard_map/all_gather | solution.py:145
  145.0 26.1 %copy.84 = bf16[1,4,7200,128]{3,1,2,0:T(4,128)(2,1)S(1)} copy(bf16[1,4,7200,128]{3,2,1,0:T(8,128)(2,1)} %bitcast.292) | data formatting | bytes 14745600
  171.1 3.0 copy-done.6
  174.0 2.0 fusion.110
  176.1 2.3 reshape.1470
  178.4 4.5 fusion.72
  183.5 7.3 multiply_convert_fusion.1
  191.8 1.9 collective-permute-start.1
  193.8 2.7 convert_reduce_fusion.3
  196.5 5.9 copy.61
  202.4 3.6 slice.212
  206.6 2.4 copy.60
  208.9 4.1 reshape.1474
  214.3 7.9 %copy.66 = bf16[5,640,640]{2,1,0:T(8,128)(2,1)} copy(bf16[5,640,640]{1,2,0:T(8,128)(2,1)} %bitcast.286) | data formatting | bytes 8192000 | tf_op jit(solution)/shard_map/transpose | solution.py:199
  222.2 2.9 fusion.90
  225.1 1.5 fusion.99
  226.6 8.0 %constant_dynamic-update-slice_fusion = bf16[1,3200,1024]{1,2,0:T(8,128)(2,1)} fusion(bf16[1,3200,1024]{1,2,0:T(8,128)(2,1)} %fusion.99, f32[640]{0:T(1024)S(1)} %add.160, f32[640]{0:T(1024)S(1)} %mul.441, f32[1024]{0:T(1024)S(1)} %add_rsqrt_fusion.1, f32[1024]{0:T(1024)S(1)} %broadcast_multiply_fusion.5, f32[640]{0:T(1024)S(1)} %add.156, ...), kind=kLoop, calls=%fused_computation.200 | loop fusion | flops 45875200 | bytes 3948032
  234.6 1.5 fusion.87
  237.5 9.6 %copy.69 = bf16[1,3200,1024]{2,1,0:T(8,128)(2,1)} copy(bf16[1,3200,1024]{1,2,0:T(8,128)(2,1)} %fusion.97) | data formatting | bytes 13107200 | tf_op jit(solution)/shard_map/concatenate | solution.py:63
  247.0 9.1 %fusion.74 = (f32[1024]{0:T(1024)S(1)}, f32[1024,640]{1,0:T(8,128)S(1)}) fusion(f32[640]{0:T(1024)S(1)} %add.163, bf16[3200,640]{1,0:T(8,128)(2,1)} %bitcast.287, bf16[1,3200,1024]{1,2,0:T(8,128)(2,1)} %fusion.97), kind=kOutput, calls=%fused_computation.148 | convolution fusion | flops 4195613696 | bytes 13277696 | tf_op jit(solution)/shard_map/co,rcl->rol/dot_general | solution.py:179
  256.7 11.8 %fusion.105 = f32[640,1280]{1,0:T(8,128)} fusion(bf16[1280,1024]{1,0:T(8,128)(2,1)} %bitcast.20, f32[640]{0:T(1024)S(1)} %add.167, f32[640]{0:T(1024)S(1)} %mul.451, f32[1024]{0:T(1024)S(1)} %add_rsqrt_fusion, f32[1024]{0:T(1024)S(1)} %broadcast_multiply_fusion.4, f32[640]{0:T(1024)S(1)} %add.163, f32[1024,640]{1,0:T(8,128)S(1)} %get-tuple-element.129), kind=kOutput, calls=%fused_computation.228 | convolution fusion | flops 1723596800 | bytes 8535552 | tf_op jit(solution)/shard_map/rhl,rdl->hd/dot_general | solution.py:187
  268.6 12.4 %fusion.50 = (f32[640]{0:T(1024)S(1)}, f32[1024]{0:T(1024)S(1)}, f32[1024]{0:T(1024)S(1)}, f32[640]{0:T(1024)S(1)}, f32[1,640,1024]{1,2,0:T(8,128)}) fusion(f32[1024]{0:T(1024)S(1)} %add_rsqrt_fusion, f32[1024]{0:T(1024)S(1)} %broadcast_multiply_fusion.4, f32[640]{0:T(1024)S(1)} %add.163, f32[1024,640]{1,0:T(8,128)S(1)} %get-tuple-element.129, ...), kind=kOutput, calls=%fused_computation.95 | convolution fusion | flops 1732113152 | bytes 9531904 | tf_op jit(solution)/shard_map/hd,rdl->rhl/dot_general | solution.py:188
  281.1 3.1 convert_reduce_fusion.1
  284.3 5.2 reshape.1493
  289.5 3.0 collective-permute-start.5
  293.9 7.6 convolution_bitcast_fusion
  301.5 9.7 %copy.71 = f32[640,5,640]{2,1,0:T(8,128)} copy(f32[640,5,640]{2,0,1:T(8,128)S(1)} %convolution_bitcast_fusion) | data formatting | bytes 16384000 | tf_op jit(solution)/shard_map/transpose | solution.py:227
  311.2 12.0 %reshape.1489 = f32[4,512000]{1,0:T(4,128)} reshape(f32[640,5,640]{2,1,0:T(8,128)} %copy.71) | data formatting | bytes 16384000 | tf_op jit(solution)/shard_map/reshape | solution.py:234
  326.9 13.5 %fusion.56 = (f32[640]{0:T(1024)S(1)}, f32[1024]{0:T(1024)S(1)}, f32[1024]{0:T(1024)S(1)}, f32[640]{0:T(1024)S(1)}, f32[1,640,1024]{1,2,0:T(8,128)}) fusion(f32[1024]{0:T(1024)S(1)} %add_rsqrt_fusion.1, f32[1024]{0:T(1024)S(1)} %broadcast_multiply_fusion.5, f32[640]{0:T(1024)S(1)} %add.156, f32[1024,640]{1,0:T(8,128)S(1)} %copy-done.2, f32[640]{0:T(1024)S(1)} %mul.441, ...), kind=kOutput, calls=%fused_computation.106 | convolution fusion | flops 4248695808 | bytes 15921664 | tf_op jit(solution)/shard_map/oc,rol->rcl/dot_general | solution.py:200
  340.5 3.3 convert_reduce_fusion.2
  343.9 6.0 fusion.57
  349.9 3.5 reshape.1484
  353.4 19.2 %multiply_reduce_fusion = (f32[1280]{0:T(1024)S(1)}, f32[1024]{0:T(1024)S(1)}, f32[1024]{0:T(1024)S(1)}, f32[1280]{0:T(1024)S(1)}, f32[1,1280,1024]{1,2,0:T(8,128)}) fusion(f32[1,1280,1024]{1,2,0:T(8,128)} %copy.61, f32[1024]{0:T(1024)S(1)} %copy-done.17, f32[1024]{0:T(1024)S(1)} %copy-done.19, f32[1280]{0:T(1024)S(1)} %copy-done.15, ...), kind=kOutput, calls=%fused_computation.24 | convolution fusion | flops 1785196032 | bytes 13471744 | tf_op jit(solution)/shard_map/dh,rhl->rdl/dot_general | solution.py:211
  374.1 1.5 dynamic-update-slice.1
  375.6 1.8 constant_dynamic-update-slice_fusion.2
  381.6 43.2 %dynamic-update-slice.6 = f32[4,923520]{1,0:T(4,128)} dynamic-update-slice(f32[4,923520]{1,0:T(4,128)} %dynamic-update-slice.5, f32[4,512000]{1,0:T(4,128)} %reshape.1489, s32[]{} %constant.29, s32[]{} %constant.35) | dynamic-update-slice | bytes 16384004
  426.2 1.6 dynamic-update-slice.8
  429.2 17.2 %dynamic-update-slice.10 = f32[4,923520]{1,0:T(4,128)} dynamic-update-slice(f32[4,923520]{1,0:T(4,128)} %dynamic-update-slice.9, f32[4,204800]{1,0:T(4,128)S(1)} %copy-done.7, s32[]{} %constant.29, s32[]{} %constant.146) | dynamic-update-slice | bytes 6553604
  447.9 12.8 %pad_bitcast_fusion = f32[1,4,7232,128]{3,1,2,0:T(4,128)} fusion(f32[4,923520]{1,0:T(4,128)} %dynamic-update-slice.11), kind=kLoop, calls=%fused_computation.1 | loop fusion | bytes 29587456
  460.6 11.4 %copy.83 = f32[1,4,7232,128]{3,2,1,0:T(8,128)} copy(f32[1,4,7232,128]{3,1,2,0:T(4,128)} %pad_bitcast_fusion) | data formatting | bytes 29622272
  472.0 24.9 %reduce-scatter.6.cloned.1.call-done = f32[4,3616,128]{2,1,0:T(8,128)} async-done(((f32[4,7232,128]{2,1,0:T(8,128)}), f32[4,3616,128]{2,1,0:T(8,128)}) %reduce-scatter.6.cloned.1.call-update) | async-done | bytes 7405584 | tf_op jit(solution)/shard_map/reduce_scatter | solution.py:244
  497.0 132.5 %reduce-scatter.8.cloned.1.call-done = f32[4,904,128]{2,1,0:T(8,128)} async-done(((f32[4,3616,128]{2,1,0:T(8,128)}), f32[4,904,128]{2,1,0:T(8,128)}) %reduce-scatter.8.cloned.1.call-update) | async-done | bytes 1851408 | tf_op jit(solution)/shard_map/reduce_scatter | solution.py:245
  629.7 5.1 copy.67
  634.7 32.4 %reduce-scatter.10.cloned.1.call-done = f32[1,904,128]{2,1,0:T(8,128)} async-done(((f32[4,904,128]{2,1,0:T(8,128)}), f32[1,904,128]{2,1,0:T(8,128)}) %reduce-scatter.10.cloned.1.call-update) | async-done | bytes 462864
  667.1 10.9 %fusion.12 = bf16[1,1280,1024]{1,2,0:T(8,128)(2,1)S(1)} fusion(f32[1,1280,1024]{1,2,0:T(8,128)} %copy.61, bf16[640,1280]{1,0:T(8,128)(2,1)} %reshape.1474, f32[1280]{0:T(1024)S(1)} %add.171, f32[640]{0:T(1024)S(1)} %add.167, f32[640]{0:T(1024)S(1)} %mul.451, f32[1024]{0:T(1024)S(1)} %add_rsqrt_fusion, f32[1024]{0:T(1024)S(1)} %broadcast_multiply_fusion.4, ...), kind=kOutput, calls=%fused_computation.18 | convolution fusion | flops 1727528960 | bytes 12145152 | tf_op jit(solution)/shard_map/hd,rhl->rdl/dot_general | solution.py:184
  679.7 2.7 copy.62
  682.4 4.6 all-to-all-start.1
  687.0 6.6 add_convert_fusion
  695.2 2.7 copy.68
  698.0 19.9 %all-to-all-done.1 = bf16[4,1,320,1024]{3,2,1,0:T(8,128)(2,1)} async-done(((bf16[4,1,320,1024]{3,2,1,0:T(8,128)(2,1)}), bf16[4,1,320,1024]{3,2,1,0:T(8,128)(2,1)}, u32[]{:S(2)}, u32[]{:S(2)}) %all-to-all-start.1) | async-done | bytes 2621472 | tf_op jit(solution)/shard_map/all_to_all | solution.py:76
  717.8 3.7 all-to-all-start.3
  721.5 29.9 %all-to-all-done.3 = bf16[4,1,320,1024]{3,2,1,0:T(8,128)(2,1)S(1)} async-done(((bf16[4,1,320,1024]{3,2,1,0:T(8,128)(2,1)}), bf16[4,1,320,1024]{3,2,1,0:T(8,128)(2,1)S(1)}, u32[]{:S(2)}, u32[]{:S(2)}) %all-to-all-start.3) | async-done | bytes 2621472 | tf_op jit(solution)/shard_map/all_to_all | solution.py:76
  751.4 3.2 slice_bitcast_fusion
  756.3 1.9 slice.231
  761.5 2.4 reshape.1496
  763.9 1.7 copy.72
  765.6 3.6 copy.108
  769.2 1.5 copy.109
  (158 shorter events, 40.1 us)
Async XLA Ops:
  7.2 137.8 %all-gather.5.cloned.1.call-start = ((), (), s32[]{:S(2)}) async-start(), calls=%async_computation.7 | async-start | bytes 9216000 | tf_op jit(solution)/shard_map/all_gather | solution.py:145
  13.2 9.0 %copy-start.24 = (f32[320]{0:T(512)S(1)}, f32[320]{0:T(512)}, u32[]{:S(2)}) copy-start(f32[320]{0:T(512)} %param.17) | copy-start | bytes 3844
  13.3 9.0 %copy-start.25 = (f32[320]{0:T(512)S(1)}, f32[320]{0:T(512)}, u32[]{:S(2)}) copy-start(f32[320]{0:T(512)} %param.18) | copy-start | bytes 3844
  13.3 9.0 %copy-start.26 = (f32[320]{0:T(512)S(1)}, f32[320]{0:T(512)}, u32[]{:S(2)}) copy-start(f32[320]{0:T(512)} %param.28) | copy-start | bytes 3844
  13.3 9.0 %copy-start.27 = (f32[160]{0:T(256)S(1)}, f32[160]{0:T(256)}, u32[]{:S(2)}) copy-start(f32[160]{0:T(256)} %param.20) | copy-start | bytes 1924
  13.3 9.0 %copy-start.28 = (f32[160]{0:T(256)S(1)}, f32[160]{0:T(256)}, u32[]{:S(2)}) copy-start(f32[160]{0:T(256)} %param.21) | copy-start | bytes 1924
  13.3 9.0 %copy-start.29 = (f32[160]{0:T(256)S(1)}, f32[160]{0:T(256)}, u32[]{:S(2)}) copy-start(f32[160]{0:T(256)} %param.22) | copy-start | bytes 1924
  13.3 9.0 %copy-start.30 = (f32[160]{0:T(256)S(1)}, f32[160]{0:T(256)}, u32[]{:S(2)}) copy-start(f32[160]{0:T(256)} %param.24) | copy-start | bytes 1924
  13.3 9.0 %copy-start.31 = (f32[160]{0:T(256)S(1)}, f32[160]{0:T(256)}, u32[]{:S(2)}) copy-start(f32[160]{0:T(256)} %param.25) | copy-start | bytes 1924
  13.3 9.0 %copy-start.32 = (f32[160]{0:T(256)S(1)}, f32[160]{0:T(256)}, u32[]{:S(2)}) copy-start(f32[160]{0:T(256)} %param.26) | copy-start | bytes 1924
  13.4 60.4 %all-to-all-start = ((bf16[4,320,1024]{2,1,0:T(8,128)(2,1)}), bf16[4,320,1024]{2,1,0:T(8,128)(2,1)S(1)}, u32[]{:S(2)}, u32[]{:S(2)}) async-start(bf16[4,320,1024]{2,1,0:T(8,128)(2,1)} %param.15), calls=%async_computation | async-start | bytes 5242880 | tf_op jit(solution)/shard_map/all_to_all | solution.py:71
  19.5 54.1 %collective-permute-start = (s32[1,64]{1,0:T(1,128)S(1)}, s32[1,64]{1,0:T(1,128)S(1)}, u32[]{:S(2)}, u32[]{:S(2)}) collective-permute-start(s32[1,64]{1,0:T(1,128)S(1)} %get-tuple-element.124), channel_id=1, source_target_pairs={{0,4},{1,5},{2,6},{3,7},{8,12},{9,13},{10,14},{11,15},{16,20},{17,... | collective-permute-start | bytes 776 | tf_op jit(solution)/shard_map/ppermute | solution.py:50
  20.9 52.6 %collective-permute-start.2 = (s32[1,64]{1,0:T(1,128)S(1)}, s32[1,64]{1,0:T(1,128)S(1)}, u32[]{:S(2)}, u32[]{:S(2)}) collective-permute-start(s32[1,64]{1,0:T(1,128)S(1)} %get-tuple-element.125), channel_id=1, source_target_pairs={{4,0},{5,1},{6,2},{7,3},{12,8},{13,9},{14,10},{15,11},{20,16},{21,... | collective-permute-start | bytes 776 | tf_op jit(solution)/shard_map/ppermute | solution.py:51
  73.1 7.3 copy-start.14
  73.6 6.9 copy-start.20
  73.7 120.1 %all-to-all-start.2 = ((bf16[4,320,1024]{2,1,0:T(8,128)(2,1)}), bf16[4,320,1024]{2,1,0:T(8,128)(2,1)}, u32[]{:S(2)}, u32[]{:S(2)}) async-start(bf16[4,320,1024]{2,1,0:T(8,128)(2,1)} %param.29), calls=%async_computation.2 | async-start | bytes 5242880 | tf_op jit(solution)/shard_map/all_to_all | solution.py:71
  78.5 418.5 %reduce-scatter.6.cloned.1.call-start = ((), (), s32[]{:S(2)}) async-start(), calls=%async_computation.8 | async-start | bytes 22216704 | tf_op jit(solution)/shard_map/reduce_scatter | solution.py:244
  79.2 2.3 copy-start
  79.6 16.6 %copy-start.16 = (f32[1024]{0:T(1024)}, f32[1024]{0:T(1024)S(1)}, u32[]{:S(2)}) copy-start(f32[1024]{0:T(1024)S(1)} %broadcast_multiply_fusion.8) | copy-start | bytes 12292
  80.4 15.8 %copy-start.18 = (f32[1024]{0:T(1024)}, f32[1024]{0:T(1024)S(1)}, u32[]{:S(2)}) copy-start(f32[1024]{0:T(1024)S(1)} %add_rsqrt_fusion.2) | copy-start | bytes 12292
  171.0 3.0 copy-start.6
  182.9 43.7 %copy-start.1 = (f32[1024,640]{1,0:T(8,128)}, f32[1024,640]{1,0:T(8,128)S(1)}, u32[]{:S(2)}) copy-start(f32[1024,640]{1,0:T(8,128)S(1)} %get-tuple-element.127) | copy-start | bytes 7864324
  190.8 1.1 copy-start.4
  191.8 30.4 %collective-permute-start.1 = (bf16[1,640,64]{1,2,0:T(8,128)(2,1)S(1)}, bf16[1,640,64]{1,2,0:T(8,128)(2,1)S(1)}, u32[]{:S(2)}, u32[]{:S(2)}) collective-permute-start(bf16[1,640,64]{1,2,0:T(8,128)(2,1)S(1)} %get-tuple-element.114), channel_id=1, source_target_pairs={{0,4},{1,5},{2,6},{3,7},{8,12},{9,13},{10,14},{11,15},{16,20},{17,... | collective-permute-start | bytes 245768 | tf_op jit(solution)/shard_map/ppermute | solution.py:50
  213.1 21.5 %collective-permute-start.3 = (bf16[1,640,64]{1,2,0:T(8,128)(2,1)S(1)}, bf16[1,640,64]{1,2,0:T(8,128)(2,1)S(1)}, u32[]{:S(2)}, u32[]{:S(2)}) collective-permute-start(bf16[1,640,64]{1,2,0:T(8,128)(2,1)S(1)} %get-tuple-element.113), channel_id=1, source_target_pairs={{4,0},{5,1},{6,2},{7,3},{12,8},{13,9},{14,10},{15,11},{20,16},{21,... | collective-permute-start | bytes 245768 | tf_op jit(solution)/shard_map/ppermute | solution.py:51
  222.2 2.9 copy-start.5
  256.2 12.4 %copy-start.8 = (f32[1024,640]{1,0:T(8,128)}, f32[1024,640]{1,0:T(8,128)S(1)}, u32[]{:S(2)}) copy-start(f32[1024,640]{1,0:T(8,128)S(1)} %get-tuple-element.129) | copy-start | bytes 7864324
  256.7 11.8 %copy-start.13 = (bf16[640,1280]{1,0:T(8,128)(2,1)S(1)}, bf16[640,1280]{1,0:T(8,128)(2,1)}, u32[]{:S(2)}) copy-start(bf16[640,1280]{1,0:T(8,128)(2,1)} %reshape.1474) | copy-start | bytes 4915204
  289.5 34.6 %collective-permute-start.5 = (bf16[1,640,64]{1,2,0:T(8,128)(2,1)S(1)}, bf16[1,640,64]{1,2,0:T(8,128)(2,1)S(1)}, u32[]{:S(2)}, u32[]{:S(2)}) collective-permute-start(bf16[1,640,64]{1,2,0:T(8,128)(2,1)S(1)} %get-tuple-element.111), channel_id=1, source_target_pairs={{0,4},{1,5},{2,6},{3,7},{8,12},{9,13},{10,14},{11,15},{16,20},{17,... | collective-permute-start | bytes 245768 | tf_op jit(solution)/shard_map/ppermute | solution.py:50
  292.6 30.6 %collective-permute-start.4 = (bf16[1,640,64]{1,2,0:T(8,128)(2,1)S(1)}, bf16[1,640,64]{1,2,0:T(8,128)(2,1)S(1)}, u32[]{:S(2)}, u32[]{:S(2)}) collective-permute-start(bf16[1,640,64]{1,2,0:T(8,128)(2,1)S(1)} %get-tuple-element.112), channel_id=1, source_target_pairs={{4,0},{5,1},{6,2},{7,3},{12,8},{13,9},{14,10},{15,11},{20,16},{21,... | collective-permute-start | bytes 245768 | tf_op jit(solution)/shard_map/ppermute | solution.py:51
  323.9 2.2 copy-start.12
  324.1 2.8 copy-start.2
  326.9 13.6 %copy-start.3 = (f32[1024,640]{1,0:T(8,128)S(1)}, f32[1024,640]{1,0:T(8,128)}, u32[]{:S(2)}) copy-start(f32[1024,640]{1,0:T(8,128)} %copy-done.1) | copy-start | bytes 7864324
  349.9 3.5 copy-start.15
  349.9 3.5 copy-start.17
  349.9 3.5 copy-start.19
  349.9 3.5 copy-start.21
  381.6 47.6 %copy-start.7 = (f32[4,204800]{1,0:T(4,128)S(1)}, f32[4,204800]{1,0:T(4,128)}, u32[]{:S(2)}) copy-start(f32[4,204800]{1,0:T(4,128)} %reshape.1493) | copy-start | bytes 9830404
  429.2 17.3 %copy-start.23 = (f32[4,320]{1,0:T(4,128)S(1)}, f32[4,320]{1,0:T(4,128)}, u32[]{:S(2)}) copy-start(f32[4,320]{1,0:T(4,128)} %convert_reduce_fusion.3) | copy-start | bytes 15364
  472.0 157.5 %reduce-scatter.8.cloned.1.call-start = ((), (), s32[]{:S(2)}) async-start(), calls=%async_computation.9 | async-start | bytes 9256960 | tf_op jit(solution)/shard_map/reduce_scatter | solution.py:245
  497.0 132.6 %copy-start.22 = (f32[4,320]{1,0:T(4,128)S(1)}, f32[4,320]{1,0:T(4,128)}, u32[]{:S(2)}) copy-start(f32[4,320]{1,0:T(4,128)} %get-tuple-element.122) | copy-start | bytes 15364
  497.0 170.1 %reduce-scatter.10.cloned.1.call-start = ((), (), s32[]{:S(2)}) async-start(), calls=%async_computation.11 | async-start | bytes 2314240
  629.5 121.9 %all-gather.7.cloned.1.call-start = ((), (), s32[]{:S(2)}) async-start(), calls=%async_computation.10 | async-start | bytes 4165632 | tf_op jit(solution)/shard_map/all_gather | solution.py:247
  629.7 37.5 %copy-start.9 = (f32[1024,640]{1,0:T(8,128)S(1)}, f32[1024,640]{1,0:T(8,128)}, u32[]{:S(2)}) copy-start(f32[1024,640]{1,0:T(8,128)} %copy-done.8) | copy-start | bytes 7864324
  682.4 35.4 %all-to-all-start.1 = ((bf16[4,1,320,1024]{3,2,1,0:T(8,128)(2,1)}), bf16[4,1,320,1024]{3,2,1,0:T(8,128)(2,1)}, u32[]{:S(2)}, u32[]{:S(2)}) async-start(bf16[4,1,320,1024]{3,2,1,0:T(8,128)(2,1)} %copy.62), calls=%async_computation.1 | async-start | bytes 5242880 | tf_op jit(solution)/shard_map/all_to_all | solution.py:76
  717.8 33.6 %all-to-all-start.3 = ((bf16[4,1,320,1024]{3,2,1,0:T(8,128)(2,1)}), bf16[4,1,320,1024]{3,2,1,0:T(8,128)(2,1)S(1)}, u32[]{:S(2)}, u32[]{:S(2)}) async-start(bf16[4,1,320,1024]{3,2,1,0:T(8,128)(2,1)} %copy.68), calls=%async_computation.3 | async-start | bytes 5242880 | tf_op jit(solution)/shard_map/all_to_all | solution.py:76
  751.4 3.2 copy-start.10
  765.6 3.6 copy-start.11
Sparse Core Ops, SparseCore 0:
  13.4 131.5 all-gather.4
  472.1 24.7 reduce-scatter.5
  499.4 130.0 reduce-scatter.7
  632.4 34.6 reduce-scatter.9
  668.5 42.8 all-gather.6
